TPU v7x, 32 devices: a whole 2x2x4 slice. The times are simulated.
32 devices in a mesh: band: 8 (over y, x, core), samp: 4 (over z).
Axes of the slice: x: 2, y: 2, z: 4, core: 2. Of those that a mesh axis runs over, the one named last changes fastest.
Arguments:
- dosage: bfloat16 [8192, 4096], P('samp', 'band'), may hold values from -1 to 2, as said below
Outputs:
- linkage: float32 [4096, 2048], P(('band', 'samp'))
Inputs may be any that keep to these rules, and one draw needn't show every extreme that they name: -1 marks a missing call; every other entry is an imputed dosage between 0 and 2.
All inputs are finite; a program needn't handle non-finite values.
Results may differ from a plain program's by a relative error of at most 0.0015.
Values may be sent and summed in bfloat16 or wider, within the bound.
A program may use at most 64 MiB of HBM per device.

v0:
```python
import jax
import jax.numpy as jnp
from jax import lax
from jax.sharding import PartitionSpec as P

TILE = 512
WIN = 2048


def passed_along(value, axis, steps):
    count = lax.axis_size(axis)
    leading, last = (max(0, -steps), min(count, count - steps))
    return lax.ppermute(value, axis, [(source, source + steps) for source in range(leading, last)])


def on_device(dosage):
    raw = dosage.astype(jnp.float32)
    observed = (raw >= 0.0).astype(jnp.float32)
    values = observed * raw
    count, total, square = lax.psum(
        (jnp.sum(observed, axis=0), jnp.sum(values, axis=0), jnp.sum(values * values, axis=0)),
        "samp",
    )
    samples = dosage.shape[0] * lax.axis_size("samp")
    mean = (total + 1.0) / (count + 1.0)
    spread = (square - 2.0 * mean * total + count * mean * mean + 0.5) / (count + 1.0)
    scaled = (observed * (values - mean) * lax.rsqrt(spread)).astype(jnp.bfloat16)
    band_width = scaled.shape[1]
    reach = (WIN - TILE + band_width - 1) // band_width
    panels = [scaled]
    for step in range(1, reach + 1):
        panels.append(passed_along(scaled, "band", -step))
    window = jnp.concatenate(panels, axis=1)
    product = lax.dot_general(
        scaled, window, (((0,), (0,)), ((), ())), preferred_element_type=jnp.float32
    )
    return lax.psum_scatter(product / samples, "samp", scatter_dimension=0, tiled=True)


def solution(mesh):
    return jax.shard_map(
        on_device,
        mesh=mesh,
        in_specs=(P("samp", "band"),),
        out_specs=P(("band", "samp"), None),
        check_vma=False,
    )
```

profile of v0, /device:TPU:3, one launch (start us, length us, event | category | flops | bytes accessed | tf_op | source)
XLA Modules:
  0.0 228.3 jit_solution(17989253486822786293)
XLA Ops:
  6.5 0.0 reduce-scatter.2.cloned.1.call-start
  6.5 2.7 %fusion.10 = (f32[512]{0:T(512)S(1)}, f32[512]{0:T(512)S(1)}, f32[512]{0:T(512)S(1)}) fusion(bf16[2048,512]{1,0:T(8,128)(2,1)} %param.1), kind=kLoop, calls=%fused_computation.12 | loop fusion | flops 8387072 | bytes 2103296 | tf_op jit(solution)/shard_map/reduce_sum | solution.py:21
  9.2 10.1 %all-reduce = (f32[512]{0:T(512)S(1)}, f32[512]{0:T(512)S(1)}, f32[512]{0:T(512)S(1)}) all-reduce(f32[512]{0:T(512)S(1)} %get-tuple-element.7, f32[512]{0:T(512)S(1)} %get-tuple-element.6, f32[512]{0:T(512)S(1)} %get-tuple-element.5), channel_id=1, replica_groups=mesh['band'=8,'samp'=4] {'samp'}, use_global_device_ids=true, to_apply=%region_3.0 | all-reduce | flops 1536 | bytes 12288 | tf_op jit(solution)/shard_map/psum | solution.py:20
  19.3 2.5 %fusion.15 = bf16[2048,512]{1,0:T(8,128)(2,1)S(1)} fusion(bf16[2048,512]{1,0:T(8,128)(2,1)} %param.1, f32[512]{0:T(512)S(1)} %get-tuple-element.12, f32[512]{0:T(512)S(1)} %get-tuple-element.11), kind=kLoop, calls=%fused_computation.17 | loop fusion | flops 7340032 | bytes 4198400 | tf_op jit(solution)/shard_map/convert_element_type | solution.py:27
  21.8 4.9 %collective-permute-start.2 = (bf16[2048,512]{1,0:T(8,128)(2,1)S(1)}, bf16[2048,512]{1,0:T(8,128)(2,1)S(1)}, u32[]{:S(2)}, u32[]{:S(2)}) collective-permute-start(bf16[2048,512]{1,0:T(8,128)(2,1)S(1)} %fusion.15), channel_id=1, source_target_pairs={{12,0},{16,4},{20,8},{24,12},{28,16},{13,1},{17,5},{21,9},{25,13},... | collective-permute-start | bytes 6291464 | tf_op jit(solution)/shard_map/ppermute | solution.py:13
  26.7 1.9 collective-permute-start.1
  28.7 1.9 collective-permute-start
  30.6 110.1 %collective-permute-done.2 = bf16[2048,512]{1,0:T(8,128)(2,1)S(1)} collective-permute-done((bf16[2048,512]{1,0:T(8,128)(2,1)S(1)}, bf16[2048,512]{1,0:T(8,128)(2,1)S(1)}, u32[]{:S(2)}, u32[]{:S(2)}) %collective-permute-start.2) | collective-permute-done | bytes 2097184 | tf_op jit(solution)/shard_map/ppermute | solution.py:13
  140.7 0.0 collective-permute-done.1
  140.7 0.0 collective-permute-done
  140.7 7.4 %fusion.17 = f32[512,2048]{1,0:T(8,128)} fusion(bf16[2048,512]{1,0:T(8,128)(2,1)S(1)} %fusion.15, bf16[2048,512]{1,0:T(8,128)(2,1)S(1)} %collective-permute-done.2, bf16[2048,512]{1,0:T(8,128)(2,1)S(1)} %collective-permute-done.1, bf16[2048,512]{1,0:T(8,128)(2,1)S(1)} %collective-permute-done), kind=kOutput, calls=%fused_computation.19 | convolution fusion | flops 4329570304 | bytes 12582912 | tf_op jit(solution)/shard_map/dot_general | solution.py:34
  148.1 0.0 reduce-scatter.2.cloned.1.call-update
  148.1 73.4 %reduce-scatter.2.cloned.1.call-done = f32[128,2048]{1,0:T(8,128)} async-done(((f32[512,2048]{1,0:T(8,128)}), f32[128,2048]{1,0:T(8,128)}) %reduce-scatter.2.cloned.1.call-update) | async-done | bytes 1048592 | tf_op jit(solution)/shard_map/reduce_scatter | solution.py:37
  (1 shorter events, 0.0 us)
Async XLA Ops:
  6.5 214.9 %reduce-scatter.2.cloned.1.call-start = ((), (), s32[]{:S(2)}) async-start(), calls=%async_computation.1 | async-start | bytes 5242880 | tf_op jit(solution)/shard_map/reduce_scatter | solution.py:37
  21.8 118.8 %collective-permute-start.2 = (bf16[2048,512]{1,0:T(8,128)(2,1)S(1)}, bf16[2048,512]{1,0:T(8,128)(2,1)S(1)}, u32[]{:S(2)}, u32[]{:S(2)}) collective-permute-start(bf16[2048,512]{1,0:T(8,128)(2,1)S(1)} %fusion.15), channel_id=1, source_target_pairs={{12,0},{16,4},{20,8},{24,12},{28,16},{13,1},{17,5},{21,9},{25,13},... | collective-permute-start | bytes 6291464 | tf_op jit(solution)/shard_map/ppermute | solution.py:13
  26.7 113.9 %collective-permute-start.1 = (bf16[2048,512]{1,0:T(8,128)(2,1)S(1)}, bf16[2048,512]{1,0:T(8,128)(2,1)S(1)}, u32[]{:S(2)}, u32[]{:S(2)}) collective-permute-start(bf16[2048,512]{1,0:T(8,128)(2,1)S(1)} %fusion.15), channel_id=1, source_target_pairs={{8,0},{12,4},{16,8},{20,12},{24,16},{28,20},{9,1},{13,5},{17,9},{2... | collective-permute-start | bytes 6291464 | tf_op jit(solution)/shard_map/ppermute | solution.py:13
  28.7 112.0 %collective-permute-start = (bf16[2048,512]{1,0:T(8,128)(2,1)S(1)}, bf16[2048,512]{1,0:T(8,128)(2,1)S(1)}, u32[]{:S(2)}, u32[]{:S(2)}) collective-permute-start(bf16[2048,512]{1,0:T(8,128)(2,1)S(1)} %fusion.15), channel_id=1, source_target_pairs={{4,0},{8,4},{12,8},{16,12},{20,16},{24,20},{28,24},{5,1},{9,5},{13... | collective-permute-start | bytes 6291464 | tf_op jit(solution)/shard_map/ppermute | solution.py:13
Sparse Core Ops, SparseCore 0:
  148.2 73.2 reduce-scatter.1
where the time goes:
time: 230 us; the launch traced here: 228 us
  waiting for transfers between devices  183 us (80%)
  between operations  13.4 us (6%)
  blocking collectives  10.1 us (4%)
  starting transfers between devices  8.73 us (4%)
  matrix products  7.4 us (3%)
  other arithmetic  5.21 us (2%)
    ppermute x3, waiting for transfers between devices, passed_along(): lax.ppermute(value, axis, [(source, source + steps) for source in range(l...  110 us
    reduce_scatter x1, waiting for transfers between devices, on_device(): lax.psum_scatter(product / samples, 'samp', scatter_dimension=0, tiled=True)  73.4 us
    psum x1, blocking collectives, on_device(): lax.psum((jnp.sum(observed, axis=0), jnp.sum(values, axis=0), jnp.sum(val...  10.1 us
    ppermute x3, starting transfers between devices, passed_along(): lax.ppermute(value, axis, [(source, source + steps) for source in range(l...  8.73 us
    dot_general x1, matrix products, on_device(): lax.dot_general(scaled, window, (((0,), (0,)), ((), ())), preferred_eleme...  7.4 us
  transfers between devices with their start and end apart: 4, of which 2 were waited for; matrix products, arithmetic and copies ran while one was open for 0% of the time, Pallas kernels for 0%

commit v1 on v0

v1 whole, which is shorter than its diff:
```python
import functools

import jax
import jax.numpy as jnp
from jax import lax
from jax.experimental import pallas as pl
from jax.experimental.pallas import tpu as pltpu
from jax.sharding import PartitionSpec as P

TILE = 512
WIN = 2048
PIECES = 2
WIRE = jnp.float32
MESH = pl.DeviceIdType.MESH


def remote(src, dst, send, recv, band, samp):
    return pltpu.make_async_remote_copy(
        src_ref=src, dst_ref=dst, send_sem=send, recv_sem=recv,
        device_id=(band, samp), device_id_type=MESH,
    )


def kernel(bands, shards, reach, samples, raw_ref, out_ref, own_t, window, stats, stats_in, coef,
           coef_in, total_ref, parts, parts_in, panel_s, panel_r, stat_s, stat_r, coef_s, coef_r,
           part_s, part_r):
    band = lax.axis_index("band")
    samp = lax.axis_index("samp")
    depth, width = raw_ref.shape
    rows = width // shards
    piece = width // PIECES
    peers = [lax.rem(samp + d, shards) for d in range(1, shards)]

    barrier = pltpu.get_barrier_semaphore()
    for peer in peers:
        pl.semaphore_signal(barrier, inc=1, device_id=(band, peer), device_id_type=MESH)
    expected = shards - 1
    for k in range(1, reach + 1):
        @pl.when(band >= k)
        def _():
            pl.semaphore_signal(barrier, inc=1, device_id=(band - k, samp), device_id_type=MESH)

        @pl.when(band + k < bands)
        def _():
            pl.semaphore_signal(barrier, inc=1, device_id=(band + k, samp), device_id_type=MESH)
    expected = expected + jnp.minimum(band, reach) + jnp.minimum(bands - 1 - band, reach)
    pl.semaphore_wait(barrier, expected)

    def panel_copy(k, j):
        columns = pl.ds(j * piece, piece)
        return remote(raw_ref.at[:, columns], window.at[k - 1, :, columns],
                      panel_s.at[k - 1, j], panel_r.at[k - 1, j], jnp.maximum(band - k, 0), samp)

    def coef_copy(k):
        return remote(coef, coef_in.at[k - 1], coef_s.at[k - 1], coef_r.at[k - 1],
                      jnp.maximum(band - k, 0), samp)

    def part_copy(k, j, d):
        columns = pl.ds(k * width + j * piece, piece)
        return remote(parts.at[pl.ds(pl.multiple_of(peers[d] * rows, rows), rows), columns],
                      parts_in.at[d, :, columns],
                      part_s.at[k, j, d], part_r.at[k, j, d], band, peers[d])

    def start_panel(k, j):
        @pl.when(band >= k)
        def _():
            panel_copy(k, j).start()

    early = [(k, 0) for k in range(1, min(reach, 2) + 1)]
    later = [(k, j) for j in range(PIECES) for k in range(1, reach + 1) if (k, j) not in early]
    for k, j in early:
        start_panel(k, j)

    step = 64

    def add(i, carry):
        x = raw_ref[pl.ds(pl.multiple_of(i * step, step), step), :].astype(jnp.float32)
        seen = jnp.where(x >= 0.0, 1.0, 0.0)
        value = jnp.where(x >= 0.0, x, 0.0)
        fold = lambda a: jnp.sum(a.reshape(step // 8, 8, width), axis=0)
        return carry[0] + fold(seen), carry[1] + fold(value), carry[2] + fold(value * value)

    zero = jnp.zeros((8, width), jnp.float32)
    sums = lax.fori_loop(0, depth // step, add, (zero, zero, zero))
    stats[...] = jnp.concatenate(
        [jnp.sum(a, axis=0, keepdims=True) for a in sums] + [jnp.zeros((5, width), jnp.float32)], axis=0
    )
    stat_copies = [
        remote(stats, stats_in.at[d], stat_s.at[d], stat_r.at[d], band, peers[d])
        for d in range(shards - 1)
    ]
    for copy in stat_copies:
        copy.start()
    for copy in stat_copies:
        copy.wait()
    sums = stats[...]
    for d in range(shards - 1):
        sums = sums + stats_in[d]
    count, total, square = sums[0:1], sums[1:2], sums[2:3]
    mean = (total + 1.0) / (count + 1.0)
    spread = (square - 2.0 * mean * total + count * mean * mean + 0.5) / (count + 1.0)
    coef[...] = jnp.concatenate(
        [mean, lax.rsqrt(spread), jnp.zeros((6, width), jnp.float32)], axis=0
    )
    for k in range(1, reach + 1):
        @pl.when(band >= k)
        def _():
            coef_copy(k).start()
    for k, j in later:
        start_panel(k, j)

    chunk = 256

    def standard(x, mean, scale):
        x = x.astype(jnp.float32)
        return jnp.where(x >= 0.0, (x - mean) * scale, 0.0).astype(jnp.bfloat16)

    own = window.at[reach]

    def scale_own(i, _):
        span = pl.ds(pl.multiple_of(i * chunk, chunk), chunk)
        scaled = standard(raw_ref[span, :], coef[0:1, :], coef[1:2, :])
        own[span, :] = scaled
        own_t[:, span] = scaled.T
        return 0

    lax.fori_loop(0, depth // chunk, scale_own, 0)

    def correlate(k, j, panel):
        columns = slice(j * piece, (j + 1) * piece)
        place = slice(k * width + j * piece, k * width + (j + 1) * piece)

        def block(i, _):
            span = pl.ds(pl.multiple_of(i * 256, 256), 256)
            total_ref[span, :] = jnp.dot(
                own_t[span, :], panel[:, columns], preferred_element_type=jnp.float32
            )
            parts[span, place] = total_ref[span, :].astype(WIRE)
            return 0

        lax.fori_loop(0, width // 256, block, 0)
        for d in range(shards - 1):
            part_copy(k, j, d).start()
        out_ref[:, place] = total_ref[pl.ds(pl.multiple_of(samp * rows, rows), rows), :]

    def finish(k, j):
        place = slice(k * width + j * piece, k * width + (j + 1) * piece)
        total = out_ref[:, place]
        for d in range(shards - 1):
            part_copy(k, j, d).wait()
            total = total + parts_in[d, :, place].astype(jnp.float32)
        out_ref[:, place] = total / samples

    for j in range(PIECES):
        correlate(0, j, own)
    for j in range(PIECES):
        for k in range(1, reach + 1):
            @pl.when(band + k < bands)
            def _():
                columns = slice(j * piece, (j + 1) * piece)
                if j == 0:
                    coef_copy(k).wait_recv()
                panel_copy(k, j).wait_recv()
                mean, scale = coef_in[k - 1, 0:1, columns], coef_in[k - 1, 1:2, columns]

                def rescale(i, _):
                    span = pl.ds(pl.multiple_of(i * chunk, chunk), chunk)
                    window[k - 1, span, columns] = standard(window[k - 1, span, columns], mean, scale)
                    return 0

                lax.fori_loop(0, depth // chunk, rescale, 0)
                correlate(k, j, window.at[k - 1])

    for j in range(PIECES):
        finish(0, j)
    for j in range(PIECES):
        for k in range(1, reach + 1):
            @pl.when(band + k < bands)
            def _():
                finish(k, j)

            @pl.when(band + k >= bands)
            def _():
                place = slice(k * width + j * piece, k * width + (j + 1) * piece)
                out_ref[:, place] = jnp.zeros((rows, piece), jnp.float32)
    for k in range(1, reach + 1):
        @pl.when(band >= k)
        def _():
            coef_copy(k).wait_send()
            for j in range(PIECES):
                panel_copy(k, j).wait_send()


def on_device(bands, shards, dosage):
    depth, width = dosage.shape
    reach = (WIN - TILE + width - 1) // width
    rows = width // shards
    f32 = jnp.float32
    dma = pltpu.SemaphoreType.DMA
    return pl.pallas_call(
        functools.partial(kernel, bands, shards, reach, depth * shards),
        out_shape=jax.ShapeDtypeStruct((rows, WIN), f32),
        in_specs=[pl.BlockSpec(memory_space=pltpu.VMEM)],
        out_specs=pl.BlockSpec(memory_space=pltpu.VMEM),
        scratch_shapes=[
            pltpu.VMEM((width, depth), jnp.bfloat16),
            pltpu.VMEM((reach + 1, depth, width), jnp.bfloat16),
            pltpu.VMEM((8, width), f32),
            pltpu.VMEM((shards - 1, 8, width), f32),
            pltpu.VMEM((8, width), f32),
            pltpu.VMEM((reach, 8, width), f32),
            pltpu.VMEM((width, width // PIECES), f32),
            pltpu.VMEM((width, WIN), WIRE),
            pltpu.VMEM((shards - 1, rows, WIN), WIRE),
            dma((reach, PIECES)), dma((reach, PIECES)),
            dma((shards - 1,)), dma((shards - 1,)),
            dma((reach,)), dma((reach,)),
            dma((reach + 1, PIECES, shards - 1)), dma((reach + 1, PIECES, shards - 1)),
        ],
        compiler_params=pltpu.CompilerParams(
            collective_id=0, has_side_effects=True, vmem_limit_bytes=48 * 1024 * 1024
        ),
    )(dosage)


def solution(mesh):
    return jax.shard_map(
        functools.partial(on_device, mesh.shape["band"], mesh.shape["samp"]),
        mesh=mesh,
        in_specs=(P("samp", "band"),),
        out_specs=P(("band", "samp"), None),
        check_vma=False,
    )
```

time: 230 us -> 136 us (0.59)
  waiting for transfers between devices: 183 us -> 0 us
  Pallas kernels: 0 us -> 133 us
  between operations: 13.4 us -> 0.01 us
  blocking collectives: 10.1 us -> 0 us
  starting transfers between devices: 8.73 us -> 0 us
  matrix products: 7.4 us -> 0 us
  other arithmetic: 5.21 us -> 0 us
  local copies, waits for them, and re-layouts: 0 us -> 2.56 us
    pallas_call x0 -> x1, Pallas kernels: none -> 133 us  [on_device(): pl.pallas_call(functools.partial(kernel, bands, shards, reach, depth * sh...]
    ppermute x3 -> x0, waiting for transfers between devices: 110 us -> none  [passed_along(): lax.ppermute(value, axis, [(source, source + steps) for source in range(l...]
    reduce_scatter x1 -> x0, waiting for transfers between devices: 73.4 us -> none  [on_device(): lax.psum_scatter(product / samples, 'samp', scatter_dimension=0, tiled=True)]
    psum x1 -> x0, blocking collectives: 10.1 us -> none  [on_device(): lax.psum((jnp.sum(observed, axis=0), jnp.sum(values, axis=0), jnp.sum(val...]
    ppermute x3 -> x0, starting transfers between devices: 8.73 us -> none  [passed_along(): lax.ppermute(value, axis, [(source, source + steps) for source in range(l...]
    dot_general x1 -> x0, matrix products: 7.4 us -> none  [on_device(): lax.dot_general(scaled, window, (((0,), (0,)), ((), ())), preferred_eleme...]
    reduce_sum x1 -> x0, other arithmetic: 2.69 us -> none  [on_device(): jnp.sum(values, axis=0)]
    unnamed x0 -> x3, local copies, waits for them, and re-layouts: none -> 2.56 us
  transfers between devices with their start and end apart: 4 -> 0, of which waited for: 2 -> 0; matrix products, arithmetic and copies ran while one was open for 0% -> 0% of each run, Pallas kernels for 0% -> 0%
where the time goes in v1:
time: 136 us
  Pallas kernels  133 us (98%)
  local copies, waits for them, and re-layouts  2.56 us (2%)
    pallas_call x1, Pallas kernels, on_device(): pl.pallas_call(functools.partial(kernel, bands, shards, reach, depth * sh...  133 us

profile of v1, /device:TPU:3, one launch (start us, length us, event | category | flops | bytes accessed | tf_op | source)
XLA Modules:
  0.0 135.6 jit_solution(2496282980625599655)
XLA Ops:
  0.0 0.0 copy-start
  0.0 1.6 %copy-done = bf16[2048,512]{1,0:T(8,128)(2,1)S(1)} copy-done((bf16[2048,512]{1,0:T(8,128)(2,1)S(1)}, bf16[2048,512]{1,0:T(8,128)(2,1)}, u32[]{:S(2)}) %copy-start) | copy-done | bytes 2097176
  1.6 133.1 %shard_map.17 = f32[128,2048]{1,0:T(8,128)S(1)} custom-call(bf16[2048,512]{1,0:T(8,128)(2,1)S(1)} %copy-done), custom_call_target="tpu_custom_call" | custom-call | tf_op jit(solution)/shard_map/pallas_call | solution.py:200
  134.7 1.0 copy.3
Async XLA Ops:
  0.0 1.6 %copy-start = (bf16[2048,512]{1,0:T(8,128)(2,1)S(1)}, bf16[2048,512]{1,0:T(8,128)(2,1)}, u32[]{:S(2)}) copy-start(bf16[2048,512]{1,0:T(8,128)(2,1)} %raw_ref.1) | copy-start | bytes 6291460

commit v2 on v1

--- a/solution.py
+++ b/solution.py
@@ -23,7 +23,7 @@
 
 def kernel(bands, shards, reach, samples, raw_ref, out_ref, own_t, window, stats, stats_in, coef,
            coef_in, total_ref, parts, parts_in, panel_s, panel_r, stat_s, stat_r, coef_s, coef_r,
-           part_s, part_r):
+           part_s, part_r, relay_s, work):
     band = lax.axis_index("band")
     samp = lax.axis_index("samp")
     depth, width = raw_ref.shape
@@ -51,22 +51,40 @@
         return remote(raw_ref.at[:, columns], window.at[k - 1, :, columns],
                       panel_s.at[k - 1, j], panel_r.at[k - 1, j], jnp.maximum(band - k, 0), samp)
 
+    even = lax.rem(band, 2) == 0
+    turn = lax.rem(band, 4)
+
+    def sends(k):
+        if k == 1:
+            return jnp.logical_not(even)
+        if k == 2:
+            return (band >= 2) & (turn != 0)
+        return even & (band >= 3)
+
+    def relay_copy(k, j):
+        columns = pl.ds(j * piece, piece)
+        onward = (k == 2) & jnp.logical_not(even)
+        target = jnp.clip(jnp.where(onward, band - 1, band + 1), 0, bands - 1)
+        slot = jnp.where(k == 3, 1, jnp.where(even, 0, 2))
+        return remote(window.at[k - 1, :, columns], window.at[slot, :, columns],
+                      relay_s.at[k - 2, j], panel_r.at[slot, j], target, samp)
+
     def coef_copy(k):
         return remote(coef, coef_in.at[k - 1], coef_s.at[k - 1], coef_r.at[k - 1],
                       jnp.maximum(band - k, 0), samp)
 
     def part_copy(k, j, d):
-        columns = pl.ds(k * width + j * piece, piece)
+        columns = pl.ds(pl.multiple_of(k * width + j * piece, piece), piece)
         return remote(parts.at[pl.ds(pl.multiple_of(peers[d] * rows, rows), rows), columns],
                       parts_in.at[d, :, columns],
                       part_s.at[k, j, d], part_r.at[k, j, d], band, peers[d])
 
     def start_panel(k, j):
-        @pl.when(band >= k)
+        @pl.when(sends(k))
         def _():
             panel_copy(k, j).start()
 
-    early = [(k, 0) for k in range(1, min(reach, 2) + 1)]
+    early = [(k, 0) for k in range(1, reach + 1)]
     later = [(k, j) for j in range(PIECES) for k in range(1, reach + 1) if (k, j) not in early]
     for k, j in early:
         start_panel(k, j)
@@ -127,13 +145,12 @@
     lax.fori_loop(0, depth // chunk, scale_own, 0)
 
     def correlate(k, j, panel):
-        columns = slice(j * piece, (j + 1) * piece)
-        place = slice(k * width + j * piece, k * width + (j + 1) * piece)
+        place = pl.ds(pl.multiple_of(k * width + j * piece, piece), piece)
 
         def block(i, _):
             span = pl.ds(pl.multiple_of(i * 256, 256), 256)
             total_ref[span, :] = jnp.dot(
-                own_t[span, :], panel[:, columns], preferred_element_type=jnp.float32
+                own_t[span, :], panel[...], preferred_element_type=jnp.float32
             )
             parts[span, place] = total_ref[span, :].astype(WIRE)
             return 0
@@ -152,24 +169,33 @@
         out_ref[:, place] = total / samples
 
     for j in range(PIECES):
-        correlate(0, j, own)
-    for j in range(PIECES):
-        for k in range(1, reach + 1):
+        correlate(0, j, own.at[:, pl.ds(j * piece, piece)])
+    for j in range(PIECES):
+        columns = slice(j * piece, (j + 1) * piece)
+        for t in range(reach):
+            late = (t + 1) % reach + 1
+            swapped = (1, 3, 2)[t]
+            k = jnp.where(even, jnp.where(turn == 2, swapped, t + 1), late)
+
             @pl.when(band + k < bands)
             def _():
-                columns = slice(j * piece, (j + 1) * piece)
+                panel_copy(k, j).wait_recv()
+
+                @pl.when((k == 2) | ((k == 3) & (turn == 1)))
+                def _():
+                    relay_copy(k, j).start()
+
                 if j == 0:
                     coef_copy(k).wait_recv()
-                panel_copy(k, j).wait_recv()
                 mean, scale = coef_in[k - 1, 0:1, columns], coef_in[k - 1, 1:2, columns]
 
                 def rescale(i, _):
                     span = pl.ds(pl.multiple_of(i * chunk, chunk), chunk)
-                    window[k - 1, span, columns] = standard(window[k - 1, span, columns], mean, scale)
+                    work[span, :] = standard(window[k - 1, span, columns], mean, scale)
                     return 0
 
                 lax.fori_loop(0, depth // chunk, rescale, 0)
-                correlate(k, j, window.at[k - 1])
+                correlate(k, j, work)
 
     for j in range(PIECES):
         finish(0, j)
@@ -187,8 +213,16 @@
         @pl.when(band >= k)
         def _():
             coef_copy(k).wait_send()
-            for j in range(PIECES):
+
+        for j in range(PIECES):
+            @pl.when(sends(k))
+            def _():
                 panel_copy(k, j).wait_send()
+
+            if k > 1:
+                @pl.when((band + k < bands) & ((k == 2) | (turn == 1)))
+                def _():
+                    relay_copy(k, j).wait_send()
 
 
 def on_device(bands, shards, dosage):
@@ -216,6 +250,8 @@
             dma((shards - 1,)), dma((shards - 1,)),
             dma((reach,)), dma((reach,)),
             dma((reach + 1, PIECES, shards - 1)), dma((reach + 1, PIECES, shards - 1)),
+            dma((reach - 1, PIECES)),
+            pltpu.VMEM((depth, width // PIECES), jnp.bfloat16),
         ],
         compiler_params=pltpu.CompilerParams(
             collective_id=0, has_side_effects=True, vmem_limit_bytes=48 * 1024 * 1024

time: 136 us -> 105 us (0.77)
  the two profiles are of different devices: /device:TPU:3 before, /device:TPU:0 now
where the time goes in v2:
time: 105 us
  Pallas kernels  103 us (98%)
  local copies, waits for them, and re-layouts  2.56 us (2%)
    pallas_call x1, Pallas kernels, on_device(): pl.pallas_call(functools.partial(kernel, bands, shards, reach, depth * sh...  103 us
    unnamed x3, local copies, waits for them, and re-layouts  2.56 us

profile of v2, /device:TPU:0, one launch (start us, length us, event | category | flops | bytes accessed | tf_op | source)
XLA Modules:
  0.0 105.1 jit_solution(16427526104910634373)
XLA Ops:
  0.0 0.0 copy-start
  0.0 1.6 %copy-done = bf16[2048,512]{1,0:T(8,128)(2,1)S(1)} copy-done((bf16[2048,512]{1,0:T(8,128)(2,1)S(1)}, bf16[2048,512]{1,0:T(8,128)(2,1)}, u32[]{:S(2)}) %copy-start) | copy-done | bytes 2097176
  1.6 102.5 %shard_map.17 = f32[128,2048]{1,0:T(8,128)S(1)} custom-call(bf16[2048,512]{1,0:T(8,128)(2,1)S(1)} %copy-done), custom_call_target="tpu_custom_call" | custom-call | tf_op jit(solution)/shard_map/pallas_call | solution.py:234
  104.1 1.0 copy.3
Async XLA Ops:
  0.0 1.6 %copy-start = (bf16[2048,512]{1,0:T(8,128)(2,1)S(1)}, bf16[2048,512]{1,0:T(8,128)(2,1)}, u32[]{:S(2)}) copy-start(bf16[2048,512]{1,0:T(8,128)(2,1)} %raw_ref.1) | copy-start | bytes 6291460

commit v3 on v2

--- a/solution.py
+++ b/solution.py
@@ -10,7 +10,6 @@
 TILE = 512
 WIN = 2048
 PIECES = 2
-WIRE = jnp.float32
 MESH = pl.DeviceIdType.MESH
 
 
@@ -22,14 +21,18 @@
 
 
 def kernel(bands, shards, reach, samples, raw_ref, out_ref, own_t, window, stats, stats_in, coef,
-           coef_in, total_ref, parts, parts_in, panel_s, panel_r, stat_s, stat_r, coef_s, coef_r,
+           coef_in, parts, far_parts, near_in, far_in, panel_s, panel_r, stat_s, stat_r, coef_s, coef_r,
            part_s, part_r, relay_s, work):
     band = lax.axis_index("band")
     samp = lax.axis_index("samp")
     depth, width = raw_ref.shape
     rows = width // shards
     piece = width // PIECES
-    peers = [lax.rem(samp + d, shards) for d in range(1, shards)]
+    half = shards // 2
+    side, seat = samp // half, lax.rem(samp, half)
+    near = [side * half + lax.rem(seat + d, half) for d in range(1, half)]
+    far = [(1 - side) * half + lax.rem(seat + d, half) for d in range(half)]
+    peers = far + near
 
     barrier = pltpu.get_barrier_semaphore()
     for peer in peers:
@@ -75,8 +78,9 @@
 
     def part_copy(k, j, d):
         columns = pl.ds(pl.multiple_of(k * width + j * piece, piece), piece)
-        return remote(parts.at[pl.ds(pl.multiple_of(peers[d] * rows, rows), rows), columns],
-                      parts_in.at[d, :, columns],
+        source, landing, slot = (far_parts, far_in, d) if d < half else (parts, near_in, d - half)
+        return remote(source.at[pl.ds(pl.multiple_of(peers[d] * rows, rows), rows), columns],
+                      landing.at[slot, :, columns],
                       part_s.at[k, j, d], part_r.at[k, j, d], band, peers[d])
 
     def start_panel(k, j):
@@ -149,23 +153,23 @@
 
         def block(i, _):
             span = pl.ds(pl.multiple_of(i * 256, 256), 256)
-            total_ref[span, :] = jnp.dot(
-                own_t[span, :], panel[...], preferred_element_type=jnp.float32
-            )
-            parts[span, place] = total_ref[span, :].astype(WIRE)
+            total = jnp.dot(own_t[span, :], panel[...], preferred_element_type=jnp.float32)
+            parts[span, place] = total
+            far_parts[span, place] = total.astype(jnp.bfloat16)
             return 0
 
         lax.fori_loop(0, width // 256, block, 0)
         for d in range(shards - 1):
             part_copy(k, j, d).start()
-        out_ref[:, place] = total_ref[pl.ds(pl.multiple_of(samp * rows, rows), rows), :]
+        out_ref[:, place] = parts[pl.ds(pl.multiple_of(samp * rows, rows), rows), place]
 
     def finish(k, j):
         place = slice(k * width + j * piece, k * width + (j + 1) * piece)
         total = out_ref[:, place]
         for d in range(shards - 1):
             part_copy(k, j, d).wait()
-            total = total + parts_in[d, :, place].astype(jnp.float32)
+            landed = far_in[d, :, place] if d < half else near_in[d - half, :, place]
+            total = total + landed.astype(jnp.float32)
         out_ref[:, place] = total / samples
 
     for j in range(PIECES):
@@ -243,9 +247,10 @@
             pltpu.VMEM((shards - 1, 8, width), f32),
             pltpu.VMEM((8, width), f32),
             pltpu.VMEM((reach, 8, width), f32),
-            pltpu.VMEM((width, width // PIECES), f32),
-            pltpu.VMEM((width, WIN), WIRE),
-            pltpu.VMEM((shards - 1, rows, WIN), WIRE),
+            pltpu.VMEM((width, WIN), f32),
+            pltpu.VMEM((width, WIN), jnp.bfloat16),
+            pltpu.VMEM((max(shards // 2 - 1, 1), rows, WIN), f32),
+            pltpu.VMEM((shards // 2, rows, WIN), jnp.bfloat16),
             dma((reach, PIECES)), dma((reach, PIECES)),
             dma((shards - 1,)), dma((shards - 1,)),
             dma((reach,)), dma((reach,)),

time: 105 us -> 77.5 us (0.74)
  the two profiles are of different devices: /device:TPU:0 before, /device:TPU:3 now
where the time goes in v3:
time: 77.5 us; the launch traced here: 77.4 us
  Pallas kernels  74.8 us (97%)
  local copies, waits for them, and re-layouts  2.56 us (3%)
    pallas_call x1, Pallas kernels, on_device(): pl.pallas_call(functools.partial(kernel, bands, shards, reach, depth * sh...  74.8 us
    unnamed x3, local copies, waits for them, and re-layouts  2.56 us

profile of v3, /device:TPU:3, one launch (start us, length us, event | category | flops | bytes accessed | tf_op | source)
XLA Modules:
  0.0 77.4 jit_solution(16459965797674229235)
XLA Ops:
  0.0 0.0 copy-start
  0.0 1.6 %copy-done = bf16[2048,512]{1,0:T(8,128)(2,1)S(1)} copy-done((bf16[2048,512]{1,0:T(8,128)(2,1)S(1)}, bf16[2048,512]{1,0:T(8,128)(2,1)}, u32[]{:S(2)}) %copy-start) | copy-done | bytes 2097176
  1.6 74.8 %shard_map.17 = f32[128,2048]{1,0:T(8,128)S(1)} custom-call(bf16[2048,512]{1,0:T(8,128)(2,1)S(1)} %copy-done), custom_call_target="tpu_custom_call" | custom-call | tf_op jit(solution)/shard_map/pallas_call | solution.py:238
  76.4 1.0 %copy.3 = f32[128,2048]{1,0:T(8,128)} copy(f32[128,2048]{1,0:T(8,128)S(1)} %shard_map.17) | data formatting | bytes 2097152
Async XLA Ops:
  0.0 1.6 %copy-start = (bf16[2048,512]{1,0:T(8,128)(2,1)S(1)}, bf16[2048,512]{1,0:T(8,128)(2,1)}, u32[]{:S(2)}) copy-start(bf16[2048,512]{1,0:T(8,128)(2,1)} %raw_ref.1) | copy-start | bytes 6291460

commit v4 on v3

--- a/solution.py
+++ b/solution.py
@@ -9,7 +9,7 @@
 
 TILE = 512
 WIN = 2048
-PIECES = 2
+PIECES = 4
 MESH = pl.DeviceIdType.MESH
 
 

time: 77.5 us -> 69.8 us (0.901)
  Pallas kernels: 74.8 us -> 67.1 us
    pallas_call x1, Pallas kernels: 74.8 us -> 67.1 us  [on_device(): pl.pallas_call(functools.partial(kernel, bands, shards, reach, depth * sh...]
where the time goes in v4:
time: 69.8 us; the launch traced here: 69.6 us
  Pallas kernels  67.1 us (96%)
  local copies, waits for them, and re-layouts  2.56 us (4%)
    pallas_call x1, Pallas kernels, on_device(): pl.pallas_call(functools.partial(kernel, bands, shards, reach, depth * sh...  67.1 us
    unnamed x3, local copies, waits for them, and re-layouts  2.56 us

profile of v4, /device:TPU:3, one launch (start us, length us, event | category | flops | bytes accessed | tf_op | source)
XLA Modules:
  0.0 69.6 jit_solution(6799686742590891209)
XLA Ops:
  0.0 0.0 copy-start
  0.0 1.6 %copy-done = bf16[2048,512]{1,0:T(8,128)(2,1)S(1)} copy-done((bf16[2048,512]{1,0:T(8,128)(2,1)S(1)}, bf16[2048,512]{1,0:T(8,128)(2,1)}, u32[]{:S(2)}) %copy-start) | copy-done | bytes 2097176
  1.6 67.1 %shard_map.17 = f32[128,2048]{1,0:T(8,128)S(1)} custom-call(bf16[2048,512]{1,0:T(8,128)(2,1)S(1)} %copy-done), custom_call_target="tpu_custom_call" | custom-call | tf_op jit(solution)/shard_map/pallas_call | solution.py:238
  68.7 1.0 %copy.3 = f32[128,2048]{1,0:T(8,128)} copy(f32[128,2048]{1,0:T(8,128)S(1)} %shard_map.17) | data formatting | bytes 2097152
Async XLA Ops:
  0.0 1.6 %copy-start = (bf16[2048,512]{1,0:T(8,128)(2,1)S(1)}, bf16[2048,512]{1,0:T(8,128)(2,1)}, u32[]{:S(2)}) copy-start(bf16[2048,512]{1,0:T(8,128)(2,1)} %raw_ref.1) | copy-start | bytes 6291460

commit v5 on v4

--- a/solution.py
+++ b/solution.py
@@ -20,12 +20,14 @@
     )
 
 
-def kernel(bands, shards, reach, samples, raw_ref, out_ref, own_t, window, stats, stats_in, coef,
+def kernel(bands, shards, reach, samples, dosage_ref, out_ref, own_t, window, stats, stats_in, coef,
            coef_in, parts, far_parts, near_in, far_in, panel_s, panel_r, stat_s, stat_r, coef_s, coef_r,
-           part_s, part_r, relay_s, work):
+           part_s, part_r, relay_s, work, raw_ref, load_s):
     band = lax.axis_index("band")
     samp = lax.axis_index("samp")
     depth, width = raw_ref.shape
+    load = pltpu.make_async_copy(dosage_ref, raw_ref, load_s)
+    load.start()
     rows = width // shards
     piece = width // PIECES
     half = shards // 2
@@ -48,9 +50,10 @@
             pl.semaphore_signal(barrier, inc=1, device_id=(band + k, samp), device_id_type=MESH)
     expected = expected + jnp.minimum(band, reach) + jnp.minimum(bands - 1 - band, reach)
     pl.semaphore_wait(barrier, expected)
+    load.wait()
 
     def panel_copy(k, j):
-        columns = pl.ds(j * piece, piece)
+        columns = pl.ds(pl.multiple_of(j * piece, piece), piece)
         return remote(raw_ref.at[:, columns], window.at[k - 1, :, columns],
                       panel_s.at[k - 1, j], panel_r.at[k - 1, j], jnp.maximum(band - k, 0), samp)
 
@@ -65,7 +68,7 @@
         return even & (band >= 3)
 
     def relay_copy(k, j):
-        columns = pl.ds(j * piece, piece)
+        columns = pl.ds(pl.multiple_of(j * piece, piece), piece)
         onward = (k == 2) & jnp.logical_not(even)
         target = jnp.clip(jnp.where(onward, band - 1, band + 1), 0, bands - 1)
         slot = jnp.where(k == 3, 1, jnp.where(even, 0, 2))
@@ -174,32 +177,38 @@
 
     for j in range(PIECES):
         correlate(0, j, own.at[:, pl.ds(j * piece, piece)])
-    for j in range(PIECES):
-        columns = slice(j * piece, (j + 1) * piece)
-        for t in range(reach):
-            late = (t + 1) % reach + 1
-            swapped = (1, 3, 2)[t]
-            k = jnp.where(even, jnp.where(turn == 2, swapped, t + 1), late)
-
-            @pl.when(band + k < bands)
-            def _():
-                panel_copy(k, j).wait_recv()
-
-                @pl.when((k == 2) | ((k == 3) & (turn == 1)))
-                def _():
-                    relay_copy(k, j).start()
-
-                if j == 0:
-                    coef_copy(k).wait_recv()
-                mean, scale = coef_in[k - 1, 0:1, columns], coef_in[k - 1, 1:2, columns]
-
-                def rescale(i, _):
-                    span = pl.ds(pl.multiple_of(i * chunk, chunk), chunk)
-                    work[span, :] = standard(window[k - 1, span, columns], mean, scale)
-                    return 0
-
-                lax.fori_loop(0, depth // chunk, rescale, 0)
-                correlate(k, j, work)
+    ahead = [(1, 0)]
+    for j in range(PIECES):
+        ahead += [(1, j + 1)] if j + 1 < PIECES else []
+        ahead += [(k, j) for k in range(2, reach + 1)]
+    level = [(k, j) for j in range(PIECES) for k in range(reach, 0, -1)]
+    for (k_even, j_even), (k_odd, j_odd) in zip(ahead, level):
+        k_relayed = k_even if k_even == 1 else reach + 2 - k_even
+        k = jnp.where(even, jnp.where(turn == 2, k_relayed, k_even), k_odd)
+        j = jnp.where(even, j_even, j_odd)
+        columns = pl.ds(pl.multiple_of(j * piece, piece), piece)
+
+        @pl.when(band + k < bands)
+        def _():
+            panel_copy(k, j).wait_recv()
+
+            @pl.when((k == 2) | ((k == 3) & (turn == 1)))
+            def _():
+                relay_copy(k, j).start()
+
+            @pl.when(j == 0)
+            def _():
+                coef_copy(k).wait_recv()
+
+            mean, scale = coef_in[k - 1, 0:1, columns], coef_in[k - 1, 1:2, columns]
+
+            def rescale(i, _):
+                span = pl.ds(pl.multiple_of(i * chunk, chunk), chunk)
+                work[span, :] = standard(window[k - 1, span, columns], mean, scale)
+                return 0
+
+            lax.fori_loop(0, depth // chunk, rescale, 0)
+            correlate(k, j, work)
 
     for j in range(PIECES):
         finish(0, j)
@@ -238,7 +247,7 @@
     return pl.pallas_call(
         functools.partial(kernel, bands, shards, reach, depth * shards),
         out_shape=jax.ShapeDtypeStruct((rows, WIN), f32),
-        in_specs=[pl.BlockSpec(memory_space=pltpu.VMEM)],
+        in_specs=[pl.BlockSpec(memory_space=pltpu.HBM)],
         out_specs=pl.BlockSpec(memory_space=pltpu.VMEM),
         scratch_shapes=[
             pltpu.VMEM((width, depth), jnp.bfloat16),
@@ -257,6 +266,8 @@
             dma((reach + 1, PIECES, shards - 1)), dma((reach + 1, PIECES, shards - 1)),
             dma((reach - 1, PIECES)),
             pltpu.VMEM((depth, width // PIECES), jnp.bfloat16),
+            pltpu.VMEM((depth, width), jnp.bfloat16),
+            dma(()),
         ],
         compiler_params=pltpu.CompilerParams(
             collective_id=0, has_side_effects=True, vmem_limit_bytes=48 * 1024 * 1024

time: 69.8 us -> 73.2 us (1.049)
  Pallas kernels: 67.1 us -> 70.4 us
    pallas_call x1, Pallas kernels: 67.1 us -> 70.4 us  [on_device(): pl.pallas_call(functools.partial(kernel, bands, shards, reach, depth * sh...]
where the time goes in v5:
time: 73.2 us; the launch traced here: 73 us
  Pallas kernels  70.4 us (96%)
  local copies, waits for them, and re-layouts  2.56 us (3%)
    pallas_call x1, Pallas kernels, on_device(): pl.pallas_call(functools.partial(kernel, bands, shards, reach, depth * sh...  70.4 us
    unnamed x3, local copies, waits for them, and re-layouts  2.56 us

profile of v5, /device:TPU:3, one launch (start us, length us, event | category | flops | bytes accessed | tf_op | source)
XLA Modules:
  0.0 73.0 jit_solution(13456960903458089306)
XLA Ops:
  0.0 0.0 copy-start
  0.0 1.6 %copy-done = bf16[2048,512]{1,0:T(8,128)(2,1)S(1)} copy-done((bf16[2048,512]{1,0:T(8,128)(2,1)S(1)}, bf16[2048,512]{1,0:T(8,128)(2,1)}, u32[]{:S(2)}) %copy-start) | copy-done | bytes 2097176
  1.6 70.4 %shard_map.17 = f32[128,2048]{1,0:T(8,128)S(1)} custom-call(bf16[2048,512]{1,0:T(8,128)(2,1)S(1)} %copy-done), custom_call_target="tpu_custom_call" | custom-call | tf_op jit(solution)/shard_map/pallas_call | solution.py:247
  72.0 1.0 %copy.3 = f32[128,2048]{1,0:T(8,128)} copy(f32[128,2048]{1,0:T(8,128)S(1)} %shard_map.17) | data formatting | bytes 2097152
Async XLA Ops:
  0.0 1.6 %copy-start = (bf16[2048,512]{1,0:T(8,128)(2,1)S(1)}, bf16[2048,512]{1,0:T(8,128)(2,1)}, u32[]{:S(2)}) copy-start(bf16[2048,512]{1,0:T(8,128)(2,1)} %dosage_ref.1) | copy-start | bytes 6291460

commit v6 on v5

--- a/solution.py
+++ b/solution.py
@@ -183,8 +183,8 @@
         ahead += [(k, j) for k in range(2, reach + 1)]
     level = [(k, j) for j in range(PIECES) for k in range(reach, 0, -1)]
     for (k_even, j_even), (k_odd, j_odd) in zip(ahead, level):
-        k_relayed = k_even if k_even == 1 else reach + 2 - k_even
-        k = jnp.where(even, jnp.where(turn == 2, k_relayed, k_even), k_odd)
+        k_last = k_odd if k_odd == 1 else reach + 2 - k_odd
+        k = jnp.where(even, k_even, jnp.where(turn == 3, k_last, k_odd))
         j = jnp.where(even, j_even, j_odd)
         columns = pl.ds(pl.multiple_of(j * piece, piece), piece)
 

time: 73.2 us -> 66 us (0.902)
  Pallas kernels: 70.4 us -> 63.3 us
    pallas_call x1, Pallas kernels: 70.4 us -> 63.3 us  [on_device(): pl.pallas_call(functools.partial(kernel, bands, shards, reach, depth * sh...]
where the time goes in v6:
time: 66 us; the launch traced here: 65.8 us
  Pallas kernels  63.3 us (96%)
  local copies, waits for them, and re-layouts  2.56 us (4%)
    pallas_call x1, Pallas kernels, on_device(): pl.pallas_call(functools.partial(kernel, bands, shards, reach, depth * sh...  63.3 us
    unnamed x3, local copies, waits for them, and re-layouts  2.56 us

profile of v6, /device:TPU:3, one launch (start us, length us, event | category | flops | bytes accessed | tf_op | source)
XLA Modules:
  0.0 65.8 jit_solution(12841479583352420720)
XLA Ops:
  0.0 0.0 copy-start
  0.0 1.6 %copy-done = bf16[2048,512]{1,0:T(8,128)(2,1)S(1)} copy-done((bf16[2048,512]{1,0:T(8,128)(2,1)S(1)}, bf16[2048,512]{1,0:T(8,128)(2,1)}, u32[]{:S(2)}) %copy-start) | copy-done | bytes 2097176
  1.6 63.3 %shard_map.17 = f32[128,2048]{1,0:T(8,128)S(1)} custom-call(bf16[2048,512]{1,0:T(8,128)(2,1)S(1)} %copy-done), custom_call_target="tpu_custom_call" | custom-call | tf_op jit(solution)/shard_map/pallas_call | solution.py:247
  64.9 1.0 %copy.3 = f32[128,2048]{1,0:T(8,128)} copy(f32[128,2048]{1,0:T(8,128)S(1)} %shard_map.17) | data formatting | bytes 2097152
Async XLA Ops:
  0.0 1.6 %copy-start = (bf16[2048,512]{1,0:T(8,128)(2,1)S(1)}, bf16[2048,512]{1,0:T(8,128)(2,1)}, u32[]{:S(2)}) copy-start(bf16[2048,512]{1,0:T(8,128)(2,1)} %dosage_ref.1) | copy-start | bytes 6291460

commit v7 on v6

--- a/solution.py
+++ b/solution.py
@@ -116,6 +116,14 @@
     ]
     for copy in stat_copies:
         copy.start()
+    chunk = 256
+
+    def turn_own(i, _):
+        span = pl.ds(pl.multiple_of(i * chunk, chunk), chunk)
+        own_t[:, span] = raw_ref[span, :].T
+        return 0
+
+    lax.fori_loop(0, depth // chunk, turn_own, 0)
     for copy in stat_copies:
         copy.wait()
     sums = stats[...]
@@ -134,19 +142,18 @@
     for k, j in later:
         start_panel(k, j)
 
-    chunk = 256
-
     def standard(x, mean, scale):
         x = x.astype(jnp.float32)
         return jnp.where(x >= 0.0, (x - mean) * scale, 0.0).astype(jnp.bfloat16)
 
     own = window.at[reach]
 
+    upright = coef[...].T
+
     def scale_own(i, _):
         span = pl.ds(pl.multiple_of(i * chunk, chunk), chunk)
-        scaled = standard(raw_ref[span, :], coef[0:1, :], coef[1:2, :])
-        own[span, :] = scaled
-        own_t[:, span] = scaled.T
+        own[span, :] = standard(raw_ref[span, :], coef[0:1, :], coef[1:2, :])
+        own_t[:, span] = standard(own_t[:, span], upright[:, 0:1], upright[:, 1:2])
         return 0
 
     lax.fori_loop(0, depth // chunk, scale_own, 0)

time: 66 us -> 66 us (level)
  no operation moved by 1% of the time
where the time goes in v7:
time: 66 us; the launch traced here: 65.8 us
  Pallas kernels  63.3 us (96%)
  local copies, waits for them, and re-layouts  2.56 us (4%)
    pallas_call x1, Pallas kernels, on_device(): pl.pallas_call(functools.partial(kernel, bands, shards, reach, depth * sh...  63.3 us
    unnamed x3, local copies, waits for them, and re-layouts  2.56 us

profile of v7, /device:TPU:3, one launch (start us, length us, event | category | flops | bytes accessed | tf_op | source)
XLA Modules:
  0.0 65.8 jit_solution(5995145711668452070)
XLA Ops:
  0.0 0.0 copy-start
  0.0 1.6 %copy-done = bf16[2048,512]{1,0:T(8,128)(2,1)S(1)} copy-done((bf16[2048,512]{1,0:T(8,128)(2,1)S(1)}, bf16[2048,512]{1,0:T(8,128)(2,1)}, u32[]{:S(2)}) %copy-start) | copy-done | bytes 2097176
  1.6 63.3 %shard_map.17 = f32[128,2048]{1,0:T(8,128)S(1)} custom-call(bf16[2048,512]{1,0:T(8,128)(2,1)S(1)} %copy-done), custom_call_target="tpu_custom_call" | custom-call | tf_op jit(solution)/shard_map/pallas_call | solution.py:254
  64.9 1.0 %copy.3 = f32[128,2048]{1,0:T(8,128)} copy(f32[128,2048]{1,0:T(8,128)S(1)} %shard_map.17) | data formatting | bytes 2097152
Async XLA Ops:
  0.0 1.6 %copy-start = (bf16[2048,512]{1,0:T(8,128)(2,1)S(1)}, bf16[2048,512]{1,0:T(8,128)(2,1)}, u32[]{:S(2)}) copy-start(bf16[2048,512]{1,0:T(8,128)(2,1)} %dosage_ref.1) | copy-start | bytes 6291460

commit v8 on v6

--- a/solution.py
+++ b/solution.py
@@ -182,7 +182,10 @@
         ahead += [(1, j + 1)] if j + 1 < PIECES else []
         ahead += [(k, j) for k in range(2, reach + 1)]
     level = [(k, j) for j in range(PIECES) for k in range(reach, 0, -1)]
-    for (k_even, j_even), (k_odd, j_odd) in zip(ahead, level):
+    for place, ((k_even, j_even), (k_odd, j_odd)) in enumerate(zip(ahead, level)):
+        if place == len(level) - reach:
+            for j in range(PIECES):
+                finish(0, j)
         k_last = k_odd if k_odd == 1 else reach + 2 - k_odd
         k = jnp.where(even, k_even, jnp.where(turn == 3, k_last, k_odd))
         j = jnp.where(even, j_even, j_odd)
@@ -210,8 +213,6 @@
             lax.fori_loop(0, depth // chunk, rescale, 0)
             correlate(k, j, work)
 
-    for j in range(PIECES):
-        finish(0, j)
     for j in range(PIECES):
         for k in range(1, reach + 1):
             @pl.when(band + k < bands)

time: 66 us -> 66 us (level)
  no operation moved by 1% of the time
where the time goes in v8:
time: 66 us; the launch traced here: 65.8 us
  Pallas kernels  63.3 us (96%)
  local copies, waits for them, and re-layouts  2.56 us (4%)
    pallas_call x1, Pallas kernels, on_device(): pl.pallas_call(functools.partial(kernel, bands, shards, reach, depth * sh...  63.3 us
    unnamed x3, local copies, waits for them, and re-layouts  2.56 us

profile of v8, /device:TPU:3, one launch (start us, length us, event | category | flops | bytes accessed | tf_op | source)
XLA Modules:
  0.0 65.8 jit_solution(16448104627134295680)
XLA Ops:
  0.0 0.0 copy-start
  0.0 1.6 %copy-done = bf16[2048,512]{1,0:T(8,128)(2,1)S(1)} copy-done((bf16[2048,512]{1,0:T(8,128)(2,1)S(1)}, bf16[2048,512]{1,0:T(8,128)(2,1)}, u32[]{:S(2)}) %copy-start) | copy-done | bytes 2097176
  1.6 63.3 %shard_map.17 = f32[128,2048]{1,0:T(8,128)S(1)} custom-call(bf16[2048,512]{1,0:T(8,128)(2,1)S(1)} %copy-done), custom_call_target="tpu_custom_call" | custom-call | tf_op jit(solution)/shard_map/pallas_call | solution.py:248
  64.9 1.0 %copy.3 = f32[128,2048]{1,0:T(8,128)} copy(f32[128,2048]{1,0:T(8,128)S(1)} %shard_map.17) | data formatting | bytes 2097152
Async XLA Ops:
  0.0 1.6 %copy-start = (bf16[2048,512]{1,0:T(8,128)(2,1)S(1)}, bf16[2048,512]{1,0:T(8,128)(2,1)}, u32[]{:S(2)}) copy-start(bf16[2048,512]{1,0:T(8,128)(2,1)} %dosage_ref.1) | copy-start | bytes 6291460
